TPU v7x, 32 devices: a whole 2x2x4 slice. The times are simulated.
32 devices in a mesh: seq: 8 (over y, x, core), exp: 4 (over z).
Axes of the slice: x: 2, y: 2, z: 4, core: 2. Of those that a mesh axis runs over, the one named last changes fastest.
Arguments:
- layer_input: bfloat16 [4, 4096, 768], P('exp', 'seq'), may hold values from -6 to 6
- token_ids: int32 [4, 4096], P('exp', 'seq'), may hold values from 0 to 8007, as said below
- segment_ids: int32 [4, 4096], P('exp'), may hold values from 0 to 7, never falling along the last dimension, each value on 1 to 1024 neighbouring positions
- hash_table: int32 [8008], replicated, may hold values from 0 to 3, as said below
- first_gain: float32 [768], replicated, may hold values from 0.25 to 1.75
- first_bias: float32 [768], replicated, may hold values from -1.5 to 1.5
- second_gain: float32 [768], replicated, may hold values from 0.25 to 1.75
- second_bias: float32 [768], replicated, may hold values from -1.5 to 1.5
- w_qkv: bfloat16 [768, 2304], replicated, may hold values from -0.21875 to 0.21875
- w_out: bfloat16 [768, 768], replicated, may hold values from -3 to 3
- w_up: bfloat16 [4, 768, 3072], P('exp'), may hold values from -0.21875 to 0.21875
- w_down: bfloat16 [4, 3072, 768], P('exp'), may hold values from -0.109375 to 0.109375
- cotangent: bfloat16 [4, 4096, 768], P('exp', 'seq'), may hold values from -6 to 6
Outputs:
- layer_output: bfloat16 [4, 4096, 768], P('exp', 'seq')
- grad_input: float32 [4, 4096, 768], P('exp', 'seq')
- grad_w_qkv: float32 [768, 2304], replicated
- grad_w_out: float32 [768, 768], replicated
- grad_first_gain: float32 [768], replicated
- grad_first_bias: float32 [768], replicated
- grad_second_gain: float32 [768], replicated
- grad_second_bias: float32 [768], replicated
- grad_w_up: float32 [4, 768, 3072], P('exp')
- grad_w_down: float32 [4, 3072, 768], P('exp')
Inputs may be any that keep to these rules, and one draw needn't show every extreme that they name: `token_ids`: token ids range over the vocabulary. Among the 512 positions that one device holds, hash_table sends exactly 256 to one expert, the same expert on all devices that hold the same positions of their sequences, and the other experts' counts differ from one another by at most one. `hash_table`: every expert is named by 2002 token ids. `segment_ids`: numbers never fall along a sequence; each document holds 1 to 1024 neighbouring positions, and one in every sequence holds exactly 1024.
All inputs are finite; a program needn't handle non-finite values.
Results may differ from a plain program's by a relative error of at most 0.017.
Values may be sent and summed in bfloat16 or wider, within the bound.
No kernel may reach another device: no remote copies, remote signals or barrier semaphores. Data moves between devices by JAX's collectives and lax.ppermute only.
A program may use at most 192 MiB of HBM per device.

v0:
```python
import math
import jax
import jax.numpy as jnp
from jax import lax
from jax.sharding import PartitionSpec as P

HEADS = 12
HEAD_DIM = 64
DOC_MOST = 1024
NEG_BIG = -1e30
EPSILON = 1e-05


def passed_along(block, axis, distance):
    devices = range(lax.axis_size(axis))
    route = [(i - distance, i) for i in devices if i - distance in devices]
    return lax.ppermute(block, axis, route)


def smooth_gate(values):
    return jax.nn.gelu(values, approximate=True)


def norm_rows(values):
    center = values - jnp.mean(values, axis=-1, keepdims=True)
    scale = lax.rsqrt(jnp.mean(center * center, axis=-1, keepdims=True) + EPSILON)
    return (center * scale, scale)


def norm_back(grad_normed, normed, scale):
    inner = jnp.mean(grad_normed * normed, axis=-1, keepdims=True)
    return scale * (grad_normed - jnp.mean(grad_normed, axis=-1, keepdims=True) - normed * inner)


def over_blocks(step, state, pieces, first):
    length = pieces[0].shape[0]
    stride = math.gcd(length, 512)

    def advance(index, current):
        begin = index * stride
        parts = tuple((piece for piece in pieces))
        return step(current, parts, first + begin)

    return lax.fori_loop(0, length // stride, advance, state)


def allowed_pairs(query_pos, query_seg, key_pos, key_seg, limit):
    inside = (key_pos[None, :] >= 0) & (query_pos[:, None] < limit)
    return (
        inside & (key_pos[None, :] <= query_pos[:, None]) & (key_seg[None, :] == query_seg[:, None])
    )


def head_split(rows):
    return rows.reshape(rows.shape[0], HEADS, HEAD_DIM)


def forward_step(queries, query_pos, query_seg, segment_row, limit):
    width = HEADS * HEAD_DIM
    scale = HEAD_DIM ** (-0.5)

    def step(state, parts, first):
        run_max, run_total, weighted = state
        count = parts[0].shape[0]
        key_rows = head_split(parts[0][:, :width])
        value_rows = head_split(parts[0][:, width:])
        key_pos = first + jnp.arange(count, dtype=jnp.int32)
        key_seg = lax.dynamic_slice_in_dim(segment_row, first, count, 0)
        allowed = allowed_pairs(query_pos, query_seg, key_pos, key_seg, limit)[None]
        scores = (
            jnp.einsum("qhd,khd->hqk", queries, key_rows, preferred_element_type=jnp.float32)
            * scale
        )
        new_max = jnp.maximum(run_max, jnp.max(jnp.where(allowed, scores, NEG_BIG), axis=-1))
        shares = jnp.where(allowed, jnp.exp(scores - new_max[..., None]), 0.0)
        factor = jnp.exp(run_max - new_max)
        run_total = run_total * factor + jnp.sum(shares, axis=-1)
        update = jnp.einsum(
            "hqk,khd->qhd",
            shares.astype(jnp.bfloat16),
            value_rows,
            preferred_element_type=jnp.float32,
        )
        weighted = weighted * factor.T[:, :, None] + update
        return (new_max, run_total, weighted)

    return step


def backward_core(queries, grad_heads, log_total, delta, key_rows, value_rows, allowed):
    scale = HEAD_DIM ** (-0.5)
    scores = (
        jnp.einsum("qhd,khd->hqk", queries, key_rows, preferred_element_type=jnp.float32) * scale
    )
    soft = jnp.where(allowed[None], jnp.exp(scores - log_total[..., None]), 0.0)
    grad_soft = jnp.einsum(
        "qhd,khd->hqk", grad_heads, value_rows, preferred_element_type=jnp.float32
    )
    grad_scores = (soft * (grad_soft - delta[..., None])).astype(jnp.bfloat16)
    return (soft.astype(jnp.bfloat16), grad_scores)


def query_step(queries, grad_heads, log_total, delta, query_pos, query_seg, segment_row, limit):
    width = HEADS * HEAD_DIM
    scale = HEAD_DIM ** (-0.5)

    def step(state, parts, first):
        count = parts[0].shape[0]
        key_rows = head_split(parts[0][:, :width])
        value_rows = head_split(parts[0][:, width:])
        key_pos = first + jnp.arange(count, dtype=jnp.int32)
        key_seg = lax.dynamic_slice_in_dim(segment_row, first, count, 0)
        allowed = allowed_pairs(query_pos, query_seg, key_pos, key_seg, limit)
        soft_low, grad_scores = backward_core(
            queries, grad_heads, log_total, delta, key_rows, value_rows, allowed
        )
        grad_query = (
            jnp.einsum("hqk,khd->qhd", grad_scores, key_rows, preferred_element_type=jnp.float32)
            * scale
        )
        grad_q, grad_block = state
        grad_keys = (
            jnp.einsum("hqk,qhd->khd", grad_scores, queries, preferred_element_type=jnp.float32)
            * scale
        )
        grad_values = jnp.einsum(
            "hqk,qhd->khd", soft_low, grad_heads, preferred_element_type=jnp.float32
        )
        joined = jnp.concatenate(
            [grad_keys.reshape(count, width), grad_values.reshape(count, width)], axis=1
        )
        current = grad_block
        grad_block = current + joined
        return (grad_q + grad_query, grad_block)

    return step


def on_device(
    layer_input,
    token_ids,
    segment_ids,
    hash_table,
    first_gain,
    first_bias,
    second_gain,
    second_bias,
    w_qkv,
    w_out,
    w_up,
    w_down,
    cotangent,
):
    local_len = layer_input.shape[1]
    width = layer_input.shape[2]
    sources = lax.axis_size("exp")
    local_exp = w_up.shape[0]
    experts_total = local_exp * sources
    capacity = 2 * local_len // experts_total
    total_len = local_len * lax.axis_size("seq")
    reach_blocks = (DOC_MOST + local_len - 2) // local_len
    offset = lax.axis_index("seq") * local_len
    segment_row = segment_ids[0]
    query_pos = offset + jnp.arange(local_len, dtype=jnp.int32)
    query_seg = lax.dynamic_slice_in_dim(segment_row, offset, local_len, 0)
    inputs = layer_input[0].astype(jnp.float32)
    normed_one, scale_one = norm_rows(inputs)
    attn_in = (normed_one * first_gain + first_bias).astype(jnp.bfloat16)
    projected = jnp.dot(attn_in, w_qkv, preferred_element_type=jnp.float32).astype(jnp.bfloat16)
    queries = head_split(projected[:, :width])
    key_value = projected[:, width:]
    kv_blocks = [key_value]
    moving = key_value
    for hop_index in range(reach_blocks):
        moving = passed_along(moving, "seq", 1)
        kv_blocks.append(moving)
    state = (
        jnp.full((HEADS, local_len), NEG_BIG, jnp.float32),
        jnp.zeros((HEADS, local_len), jnp.float32),
        jnp.zeros((local_len, HEADS, HEAD_DIM), jnp.float32),
    )
    attend = forward_step(queries, query_pos, query_seg, segment_row, total_len)
    for block_index in range(reach_blocks + 1):
        state = over_blocks(
            attend, state, (kv_blocks[block_index],), offset - block_index * local_len
        )
    run_max, run_total, weighted = state
    attn_exact = (weighted / run_total.T[:, :, None]).reshape(local_len, width)
    log_total = run_max + jnp.log(run_total)
    attn_rows = attn_exact.astype(jnp.bfloat16)
    resid = inputs + jnp.dot(attn_rows, w_out, preferred_element_type=jnp.float32)
    normed_two, scale_two = norm_rows(resid)
    ffn_in = (normed_two * second_gain + second_bias).astype(jnp.bfloat16)
    choice_ids = hash_table[token_ids[0]]
    order = jnp.argsort(choice_ids, stable=True)
    places = jnp.argsort(order, stable=True)
    expert_grid = jnp.arange(experts_total, dtype=jnp.int32)
    matches = choice_ids[:, None] == expert_grid[None, :]
    counts = jnp.sum(matches.astype(jnp.int32), axis=0)
    starts = jnp.cumsum(counts) - counts
    slot_grid = jnp.arange(capacity, dtype=jnp.int32)
    gather_index = order[jnp.minimum(starts[:, None] + slot_grid[None, :], local_len - 1)]
    filled = (slot_grid[None, :] < counts[:, None])[:, :, None]
    own_start = jnp.sum(jnp.where(matches, starts[None, :], 0), axis=1)
    token_slot = choice_ids * capacity + places - own_start
    send = jnp.where(filled, ffn_in[gather_index], jnp.zeros((), jnp.bfloat16))
    received = lax.all_to_all(send, "exp", split_axis=0, concat_axis=0, tiled=True)
    grouped = received.reshape(sources, local_exp, capacity, width)
    pre_act = jnp.einsum("secd,edf->secf", grouped, w_up, preferred_element_type=jnp.float32)
    activated, gate_pullback = jax.vjp(smooth_gate, pre_act)
    hidden = activated.astype(jnp.bfloat16)
    expert_out = jnp.einsum(
        "secf,efd->secd", hidden, w_down, preferred_element_type=jnp.float32
    ).astype(jnp.bfloat16)
    returned = lax.all_to_all(
        expert_out.reshape(experts_total, capacity, width),
        "exp",
        split_axis=0,
        concat_axis=0,
        tiled=True,
    )
    ffn_rows = returned.reshape(experts_total * capacity, width)[token_slot].astype(jnp.float32)
    layer_output = (resid + ffn_rows).astype(jnp.bfloat16)
    grad_final = cotangent[0].astype(jnp.float32)
    grad_branch = grad_final.astype(jnp.bfloat16)
    grad_send = jnp.where(filled, grad_branch[gather_index], jnp.zeros((), jnp.bfloat16))
    grad_received = lax.all_to_all(
        grad_send, "exp", split_axis=0, concat_axis=0, tiled=True
    ).reshape(sources, local_exp, capacity, width)
    grad_w_down = jnp.einsum(
        "secf,secd->efd", hidden, grad_received, preferred_element_type=jnp.float32
    )
    grad_hidden = jnp.einsum(
        "secd,efd->secf", grad_received, w_down, preferred_element_type=jnp.float32
    )
    grad_pre = gate_pullback(grad_hidden)[0].astype(jnp.bfloat16)
    grad_w_up = jnp.einsum("secd,secf->edf", grouped, grad_pre, preferred_element_type=jnp.float32)
    grad_slots = jnp.einsum(
        "secf,edf->secd", grad_pre, w_up, preferred_element_type=jnp.float32
    ).astype(jnp.bfloat16)
    grad_back = lax.all_to_all(
        grad_slots.reshape(experts_total, capacity, width),
        "exp",
        split_axis=0,
        concat_axis=0,
        tiled=True,
    )
    grad_ffn_in = grad_back.reshape(experts_total * capacity, width)[token_slot].astype(jnp.float32)
    grad_second_gain = jnp.sum(grad_ffn_in * normed_two, axis=0)
    grad_second_bias = jnp.sum(grad_ffn_in, axis=0)
    grad_resid = grad_final + norm_back(grad_ffn_in * second_gain, normed_two, scale_two)
    grad_attn = grad_resid.astype(jnp.bfloat16)
    grad_w_out = jnp.einsum("cd,ce->de", attn_rows, grad_attn, preferred_element_type=jnp.float32)
    grad_out_rows = jnp.einsum(
        "ce,de->cd", grad_attn, w_out, preferred_element_type=jnp.float32
    ).astype(jnp.bfloat16)
    grad_heads = head_split(grad_out_rows)
    delta = jnp.sum(grad_heads.astype(jnp.float32) * head_split(attn_exact), axis=-1).T
    back_blocks = [key_value]
    moving = key_value
    for hop_index in range(reach_blocks):
        moving = passed_along(moving, "seq", 1)
        back_blocks.append(moving)
    grad_query = jnp.zeros((local_len, HEADS, HEAD_DIM), jnp.float32)
    block_grads = []
    for block_index in range(reach_blocks + 1):
        base = offset - block_index * local_len
        back_step = query_step(
            queries, grad_heads, log_total, delta, query_pos, query_seg, segment_row, total_len
        )
        grad_query, grad_block = over_blocks(
            back_step,
            (grad_query, jnp.zeros((local_len, 2 * width), jnp.float32)),
            (back_blocks[block_index],),
            base,
        )
        block_grads.append(grad_block)
    carried = block_grads[reach_blocks]
    for block_index in range(reach_blocks, 0, -1):
        carried = (
            passed_along(carried.astype(jnp.bfloat16), "seq", -1).astype(carried.dtype)
            + block_grads[block_index - 1]
        )
    grad_proj = jnp.concatenate([grad_query.reshape(local_len, width), carried], axis=1).astype(
        jnp.bfloat16
    )
    grad_w_qkv = jnp.einsum("cd,ce->de", attn_in, grad_proj, preferred_element_type=jnp.float32)
    grad_attn_in = jnp.einsum("ce,de->cd", grad_proj, w_qkv, preferred_element_type=jnp.float32)
    grad_first_gain = jnp.sum(grad_attn_in * normed_one, axis=0)
    grad_first_bias = jnp.sum(grad_attn_in, axis=0)
    grad_input = grad_resid + norm_back(grad_attn_in * first_gain, normed_one, scale_one)
    dense = lax.psum(
        (
            grad_w_qkv,
            grad_w_out,
            grad_first_gain,
            grad_first_bias,
            grad_second_gain,
            grad_second_bias,
        ),
        ("seq", "exp"),
    )
    expert_sums = (
        lax.psum(grad_w_up.astype(jnp.bfloat16), "seq").astype(jnp.float32),
        lax.psum(grad_w_down.astype(jnp.bfloat16), "seq").astype(jnp.float32),
    )
    return (
        layer_output[None],
        grad_input[None],
        dense[0],
        dense[1],
        dense[2],
        dense[3],
        dense[4],
        dense[5],
        expert_sums[0],
        expert_sums[1],
    )


def solution(mesh):
    in_specs = (
        P("exp", "seq", None),
        P("exp", "seq"),
        P("exp", None),
        P(),
        P(),
        P(),
        P(),
        P(),
        P(),
        P(),
        P("exp", None, None),
        P("exp", None, None),
        P("exp", "seq", None),
    )
    out_specs = (
        P("exp", "seq", None),
        P("exp", "seq", None),
        P(),
        P(),
        P(),
        P(),
        P(),
        P(),
        P("exp", None, None),
        P("exp", None, None),
    )
    return jax.shard_map(
        on_device, mesh=mesh, in_specs=in_specs, out_specs=out_specs, check_vma=False
    )
```

profile of v0, /device:TPU:0, one launch (start us, length us, event | category | flops | bytes accessed | tf_op | source)
XLA Modules:
  0.0 691.7 jit_solution(2766946564341442537)
XLA Ops:
  27.7 11.3 %gather_fusion.1 = s32[1024]{0:T(1024)} fusion(s32[512]{0:T(512)S(1)} %get-tuple-element.163, s32[1024]{0:T(1024)S(1)} %broadcast_clamp_fusion.1), kind=kCustom, calls=%fused_computation.1 | custom fusion | bytes 12288 | tf_op jit(solution)/shard_map/gather | solution.py:202
  58.6 7.0 %gather_fusion.4 = bf16[1024,768]{1,0:T(8,128)(2,1)} fusion(bf16[512,768]{1,0:T(8,128)(2,1)} %bitcast.289, s32[1024]{0:T(1024)S(1)} %broadcast_clamp_fusion), kind=kCustom, calls=%fused_computation.4 | custom fusion | bytes 3149824 | tf_op jit(solution)/shard_map/gather | solution.py:226
  65.6 8.6 %select_reduce_fusion.2 = (f32[12,512]{1,0:T(8,128)}, f32[12,512,512]{1,2,0:T(8,128)}) fusion(pred[512,512]{0,1:T(8,128)(4,1)} %get-tuple-element.239, bf16[512,12,64]{0,2,1:T(8,128)(2,1)} %bitcast.294, bf16[512,12,64]{0,2,1:T(8,128)(2,1)} %bitcast.302), kind=kOutput, calls=%fused_computation.33 | convolution fusion | flops 412084224 | bytes 14442496 | tf_op jit(solution)/shard_map/while/body/eval_jaxpr/qhd,khd->hqk/dot_general | solution.py:71
  81.5 8.6 %select_reduce_fusion.1 = (f32[12,512]{1,0:T(8,128)}, f32[12,512,512]{1,2,0:T(8,128)}) fusion(pred[512,512]{0,1:T(8,128)(4,1)} %get-tuple-element.241, bf16[512,12,64]{0,2,1:T(8,128)(2,1)} %bitcast.295, bf16[512,12,64]{0,2,1:T(8,128)(2,1)} %bitcast.300), kind=kOutput, calls=%fused_computation.31 | convolution fusion | flops 412084224 | bytes 14442496 | tf_op jit(solution)/shard_map/while/body/eval_jaxpr/qhd,khd->hqk/dot_general | solution.py:71
  97.3 8.1 %select_reduce_fusion = (f32[12,512]{1,0:T(8,128)S(1)}, f32[12,512,512]{1,2,0:T(8,128)}) fusion(pred[512,512]{0,1:T(8,128)(4,1)} %get-tuple-element.240, bf16[512,12,64]{0,2,1:T(8,128)(2,1)} %bitcast.296, bf16[512,12,64]{0,2,1:T(8,128)(2,1)} %bitcast.304), kind=kOutput, calls=%fused_computation.29 | convolution fusion | flops 412084224 | bytes 14442496 | tf_op jit(solution)/shard_map/while/body/eval_jaxpr/qhd,khd->hqk/dot_general | solution.py:71
  106.1 7.3 %fusion.13 = f32[12,512]{1,0:T(8,128)S(1)} fusion(f32[12,512,512]{1,2,0:T(8,128)} %get-tuple-element.247, f32[12,512]{1,0:T(8,128)S(1)} %get-tuple-element.210, pred[512,512]{0,1:T(8,128)(4,1)S(1)} %copy-done.19), kind=kLoop, calls=%fused_computation.36 | loop fusion | flops 12576768 | bytes 12894208 | tf_op jit(solution)/shard_map/while/body/eval_jaxpr/reduce_sum | solution.py:77
  113.4 20.8 %fusion.36 = f32[12,64,512]{2,1,0:T(8,128)} fusion(bf16[512,12,64]{0,2,1:T(8,128)(2,1)} %bitcast.324, f32[12,512,512]{1,2,0:T(8,128)} %get-tuple-element.247, f32[12,512]{1,0:T(8,128)S(1)} %get-tuple-element.210, pred[512,512]{0,1:T(8,128)(4,1)} %get-tuple-element.241), kind=kOutput, calls=%fused_computation.57 | convolution fusion | flops 415236096 | bytes 15228928 | tf_op jit(solution)/shard_map/while/body/eval_jaxpr/hqk,khd->qhd/dot_general | solution.py:78
  142.5 7.3 %fusion.15 = f32[12,512]{1,0:T(8,128)S(1)} fusion(f32[12,512,512]{1,2,0:T(8,128)} %get-tuple-element.245, f32[12,512]{1,0:T(8,128)} %get-tuple-element.196, pred[512,512]{0,1:T(8,128)(4,1)} %get-tuple-element.240), kind=kLoop, calls=%fused_computation.38 | loop fusion | flops 12576768 | bytes 12894208 | tf_op jit(solution)/shard_map/while/body/eval_jaxpr/reduce_sum | solution.py:77
  150.0 8.8 %fusion.158 = (bf16[512,12,64]{0,2,1:T(8,128)(2,1)S(1)}, f32[512,12,64]{0,2,1:T(8,128)}) fusion(f32[512,12]{0,1:T(8,128)S(1)} %get-tuple-element.194, bf16[512,12,64]{0,2,1:T(8,128)(2,1)S(1)} %bitcast.326, f32[12,512,512]{1,2,0:T(8,128)} %get-tuple-element.245, f32[12,512]{1,0:T(8,128)S(1)} %copy-done.37, pred[512,512]{0,1:T(8,128)(4,1)S(1)} %copy-done.21, ...), kind=kOutput, calls=%fused_computation.216 | convolution fusion | flops 417988608 | bytes 19259392 | tf_op jit(solution)/shard_map/while/body/eval_jaxpr/hqk,khd->qhd/dot_general | solution.py:78
  162.6 7.0 %gather_fusion.2 = bf16[1024,768]{1,0:T(8,128)(2,1)} fusion(bf16[512,768]{1,0:T(8,128)(2,1)} %add_convert_fusion.1, s32[1024]{0:T(1024)} %copy-done.44), kind=kCustom, calls=%fused_computation.2 | custom fusion | bytes 3149824 | tf_op jit(solution)/shard_map/gather | solution.py:206
  173.5 4.9 all-to-all-start
  186.3 28.2 %all-to-all-done = bf16[4,256,768]{2,1,0:T(8,128)(2,1)} async-done(((bf16[4,256,768]{2,1,0:T(8,128)(2,1)}), bf16[4,256,768]{2,1,0:T(8,128)(2,1)}, u32[]{:S(2)}, u32[]{:S(2)}) %all-to-all-start) | async-done | bytes 1572896 | tf_op jit(solution)/shard_map/all_to_all | solution.py:207
  218.9 7.4 %fusion.54 = f32[4,256,3072]{2,1,0:T(8,128)S(1)} fusion(bf16[4,256,768]{2,1,0:T(8,128)(2,1)} %all-to-all-done, bf16[1,768,3072]{2,1,0:T(8,128)(2,1)} %param.23), kind=kOutput, calls=%fused_computation.69 | convolution fusion | flops 4831838208 | bytes 18874368 | tf_op jit(solution)/shard_map/secd,edf->secf/dot_general | solution.py:209
  230.7 10.8 %fusion.77 = bf16[4,256,768]{2,1,0:T(8,128)(2,1)} fusion(bf16[1,3072,768]{2,1,0:T(8,128)(2,1)} %param.24, f32[4,256,3072]{2,1,0:T(8,128)S(1)} %fusion.54), kind=kOutput, calls=%fused_computation.95 | convolution fusion | flops 4860936192 | bytes 18874368 | tf_op jit(solution)/shard_map/secf,efd->secd/dot_general | solution.py:212
  241.5 13.9 %all-to-all-done.2 = bf16[4,256,768]{2,1,0:T(8,128)(2,1)} async-done(((bf16[4,256,768]{2,1,0:T(8,128)(2,1)}), bf16[4,256,768]{2,1,0:T(8,128)(2,1)}, u32[]{:S(2)}, u32[]{:S(2)}) %all-to-all-start.2) | async-done | bytes 1572896 | tf_op jit(solution)/shard_map/all_to_all | solution.py:227
  260.2 15.3 %fusion.6 = bf16[4,1,256,3072]{3,2,0,1:T(8,128)(2,1)S(1)} fusion(f32[4,256,3072]{2,1,0:T(8,128)} %copy-done.64, bf16[4,256,768]{2,1,0:T(8,128)(2,1)} %all-to-all-done.2, bf16[1,3072,768]{2,1,0:T(8,128)(2,1)} %param.24), kind=kOutput, calls=%fused_computation.14 | convolution fusion | flops 4894752768 | bytes 25165824 | tf_op jit(solution)/shard_map/secd,efd->secf/dot_general | solution.py:233
  275.5 8.5 %fusion.82 = bf16[4,256,768]{2,1,0:T(8,128)(2,1)} fusion(bf16[1,768,3072]{2,1,0:T(8,128)(2,1)} %param.23, bf16[4,1,256,3072]{3,2,0,1:T(8,128)(2,1)S(1)} %fusion.6), kind=kOutput, calls=%fused_computation.96 | convolution fusion | flops 4832624640 | bytes 12582912 | tf_op jit(solution)/shard_map/secf,edf->secd/dot_general | solution.py:238
  284.1 8.2 %fusion.56 = bf16[1,768,3072]{2,1,0:T(8,128)(2,1)} fusion(bf16[4,256,768]{2,1,0:T(8,128)(2,1)} %all-to-all-done, bf16[4,1,256,3072]{3,2,0,1:T(8,128)(2,1)S(1)} %fusion.6), kind=kOutput, calls=%fused_computation.71 | convolution fusion | flops 4834197504 | bytes 12582912 | tf_op jit(solution)/shard_map/secd,secf->edf/dot_general | solution.py:237
  301.1 12.0 %fusion.59 = bf16[1,3072,768]{2,1,0:T(8,128)(2,1)} fusion(bf16[4,256,768]{2,1,0:T(8,128)(2,1)} %all-to-all-done.2, f32[4,256,3072]{2,1,0:T(8,128)} %copy-done.64), kind=kOutput, calls=%fused_computation.72 | convolution fusion | flops 4862509056 | bytes 18874368 | tf_op jit(solution)/shard_map/secf,secd->efd/dot_general | solution.py:230
  318.1 19.5 %all-to-all-done.3 = bf16[4,256,768]{2,1,0:T(8,128)(2,1)} async-done(((bf16[4,256,768]{2,1,0:T(8,128)(2,1)}), bf16[4,256,768]{2,1,0:T(8,128)(2,1)}, u32[]{:S(2)}, u32[]{:S(2)}) %all-to-all-start.3) | async-done | bytes 1572896 | tf_op jit(solution)/shard_map/all_to_all | solution.py:241
  356.2 8.6 %fusion.110 = bf16[12,64,512]{2,1,0:T(8,128)(2,1)} fusion(bf16[512,12,64]{0,2,1:T(8,128)(2,1)} %bitcast.311, f32[12,512,512]{1,2,0:T(8,128)} %get-tuple-element.245, f32[12,512]{1,0:T(8,128)} %log_add_fusion, pred[512,512]{0,1:T(8,128)(4,1)} %get-tuple-element.240), kind=kOutput, calls=%fused_computation.132 | convolution fusion | flops 415629312 | bytes 14442496 | tf_op jit(solution)/shard_map/while/body/eval_jaxpr/hqk,qhd->khd/dot_general | solution.py:126
  364.8 7.8 %multiply_convert_fusion = bf16[12,512,512]{1,2,0:T(8,128)(2,1)S(1)} fusion(f32[12,512,512]{1,2,0:T(8,128)} %get-tuple-element.245, f32[12,512]{1,0:T(8,128)S(1)} %bitcast.331, f32[12,512]{1,0:T(8,128)S(1)} %copy-done.47, pred[512,512]{0,1:T(8,128)(4,1)S(1)} %copy-done.22, bf16[512,12,64]{0,2,1:T(8,128)(2,1)S(1)} %bitcast.312, ...), kind=kOutput, calls=%fused_computation.22 | convolution fusion | flops 421527552 | bytes 20758528 | tf_op jit(solution)/shard_map/while/body/eval_jaxpr/qhd,khd->hqk/dot_general | solution.py:96
  372.7 7.6 %multiply_convert_fusion.2 = bf16[12,512,512]{1,2,0:T(8,128)(2,1)S(1)} fusion(f32[12,512,512]{1,2,0:T(8,128)} %get-tuple-element.262, f32[12,512]{1,0:T(8,128)S(1)} %bitcast.332, f32[12,512]{1,0:T(8,128)S(1)} %copy-done.47, pred[512,512]{0,1:T(8,128)(4,1)} %get-tuple-element.239, bf16[512,12,64]{0,2,1:T(8,128)(2,1)S(1)} %bitcast.313, ...), kind=kOutput, calls=%fused_computation.26 | convolution fusion | flops 421527552 | bytes 20758528 | tf_op jit(solution)/shard_map/while/body/eval_jaxpr/qhd,khd->hqk/dot_general | solution.py:96
  385.8 8.0 %multiply_convert_fusion.1 = bf16[12,512,512]{1,2,0:T(8,128)(2,1)S(1)} fusion(f32[12,512,512]{1,2,0:T(8,128)} %get-tuple-element.247, f32[12,512]{1,0:T(8,128)S(1)} %bitcast.333, f32[12,512]{1,0:T(8,128)S(1)} %copy-done.47, pred[512,512]{0,1:T(8,128)(4,1)} %get-tuple-element.241, bf16[512,12,64]{0,2,1:T(8,128)(2,1)S(1)} %bitcast.314, ...), kind=kOutput, calls=%fused_computation.24 | convolution fusion | flops 421527552 | bytes 20758528 | tf_op jit(solution)/shard_map/while/body/eval_jaxpr/qhd,khd->hqk/dot_general | solution.py:96
  404.0 6.1 fusion.30
  423.5 14.7 %collective-permute-done.3 = bf16[512,1536]{0,1:T(8,128)(2,1)} collective-permute-done((bf16[512,1536]{0,1:T(8,128)(2,1)}, bf16[512,1536]{0,1:T(8,128)(2,1)}, u32[]{:S(2)}, u32[]{:S(2)}) %collective-permute-start.3) | collective-permute-done | bytes 1572896 | tf_op jit(solution)/shard_map/ppermute | solution.py:17
  441.4 5.3 fusion.106
  446.7 23.3 %all-reduce.8.cloned.1.call-done = (bf16[1,768,3072]{2,1,0:T(8,128)(2,1)}, bf16[1,3072,768]{2,1,0:T(8,128)(2,1)}) async-done(((bf16[1,768,3072]{2,1,0:T(8,128)(2,1)}, bf16[1,3072,768]{2,1,0:T(8,128)(2,1)}), (bf16[1,768,3072]{2,1,0:T(8,128)(2,1)}, bf16[1,3072,768]{2,1,0:T(8,128)(2,1)})) %all-reduce.8.cloned.1.call-update) | async-done | bytes 9437200 | tf_op jit(solution)/shard_map/psum | solution.py:304
  470.0 7.5 %convert_element_type.162 = f32[1,768,3072]{2,1,0:T(8,128)} convert(bf16[1,768,3072]{2,1,0:T(8,128)(2,1)} %get-tuple-element.192) | non-fusion elementwise | flops 2359296 | bytes 14155776 | tf_op jit(solution)/shard_map/convert_element_type | solution.py:304
  486.2 55.8 %all-reduce = (f32[768]{0:T(1024)}, f32[768]{0:T(1024)}, f32[768]{0:T(1024)}, f32[768]{0:T(1024)}) all-reduce(f32[768]{0:T(1024)} %get-tuple-element.167, f32[768]{0:T(1024)} %get-tuple-element.170, f32[768]{0:T(1024)S(1)} %get-tuple-element.165, f32[768]{0:T(1024)S(1)} %copy-done.50), channel_id=1, replica_groups=mesh['seq'=8,'exp'=4] {'seq','exp'}, use_global_device_ids=true, to_apply=%region_23.24 | all-reduce | flops 3072 | bytes 24576 | tf_op jit(solution)/shard_map/psum | solution.py:292
  547.3 129.1 %all-reduce.6.cloned.1.call-done = (f32[768,2304]{1,0:T(8,128)}, f32[768,768]{1,0:T(8,128)}) async-done(((f32[768,2304]{1,0:T(8,128)}, f32[768,768]{1,0:T(8,128)}), (f32[768,2304]{1,0:T(8,128)}, f32[768,768]{1,0:T(8,128)})) %all-reduce.6.cloned.1.call-update) | async-done | bytes 9437200 | tf_op jit(solution)/shard_map/psum | solution.py:292
  676.4 6.6 copy.132
  (239 shorter events, 172.4 us)
Async XLA Ops:
  10.2 9.6 %copy-start.57 = (s32[1,512]{1,0:T(1,128)S(1)}, s32[1,512]{1,0:T(1,128)}, u32[]{:S(2)}) copy-start(s32[1,512]{1,0:T(1,128)} %param.14) | copy-start | bytes 6148
  16.2 29.7 %collective-permute-start = (bf16[512,1536]{1,0:T(8,128)(2,1)}, bf16[512,1536]{1,0:T(8,128)(2,1)}, u32[]{:S(2)}, u32[]{:S(2)}) collective-permute-start(bf16[512,1536]{1,0:T(8,128)(2,1)} %slice.67), channel_id=1, source_target_pairs={{0,4},{4,8},{8,12},{12,16},{16,20},{20,24},{24,28},{1,5},{5,9},{9,... | collective-permute-start | bytes 4718600 | tf_op jit(solution)/shard_map/ppermute | solution.py:17
  40.5 18.1 %copy-start.44 = (s32[1024]{0:T(1024)}, s32[1024]{0:T(1024)S(1)}, u32[]{:S(2)}) copy-start(s32[1024]{0:T(1024)S(1)} %broadcast_clamp_fusion) | copy-start | bytes 12292
  45.9 44.2 %collective-permute-start.1 = (bf16[512,1536]{1,0:T(8,128)(2,1)}, bf16[512,1536]{1,0:T(8,128)(2,1)}, u32[]{:S(2)}, u32[]{:S(2)}) collective-permute-start(bf16[512,1536]{1,0:T(8,128)(2,1)} %collective-permute-done), channel_id=1, source_target_pairs={{0,4},{4,8},{8,12},{12,16},{16,20},{20,24},{24,28},{1,5},{5,9},{9,... | collective-permute-start | bytes 4718600 | tf_op jit(solution)/shard_map/ppermute | solution.py:17
  97.3 8.8 %copy-start.19 = (pred[512,512]{0,1:T(8,128)(4,1)S(1)}, pred[512,512]{0,1:T(8,128)(4,1)}, u32[]{:S(2)}) copy-start(pred[512,512]{0,1:T(8,128)(4,1)} %get-tuple-element.241) | copy-start | bytes 786436
  106.1 28.1 %slice-start = ((s8[12582912]{0:T(1024)(128)(4,1)}), s8[4194304]{0:T(1024)(128)(4,1)S(1)}, s32[]{:S(2)}) async-start(s8[12582912]{0:T(1024)(128)(4,1)} %bitcast.290), calls=%async_computation.6 | async-start | bytes 8388608
  106.1 28.1 %slice-start.1 = ((s8[12582912]{0:T(1024)(128)(4,1)}), s8[4194304]{0:T(1024)(128)(4,1)S(1)}, s32[]{:S(2)}) async-start(s8[12582912]{0:T(1024)(128)(4,1)} %bitcast.290), calls=%async_computation.7 | async-start | bytes 8388608
  113.4 36.4 %copy-start.34 = (f32[12,512]{1,0:T(8,128)}, f32[12,512]{1,0:T(8,128)S(1)}, u32[]{:S(2)}) copy-start(f32[12,512]{1,0:T(8,128)S(1)} %fusion.13) | copy-start | bytes 73732
  113.4 20.8 %slice-start.2 = ((s8[12582912]{0:T(1024)(128)(4,1)}), s8[4194304]{0:T(1024)(128)(4,1)S(1)}, s32[]{:S(2)}) async-start(s8[12582912]{0:T(1024)(128)(4,1)} %bitcast.290), calls=%async_computation.8 | async-start | bytes 8388608
  137.8 12.1 %copy-start.35 = (f32[12,512]{1,0:T(8,128)}, f32[12,512]{1,0:T(8,128)S(1)}, u32[]{:S(2)}) copy-start(f32[12,512]{1,0:T(8,128)S(1)} %fusion.11) | copy-start | bytes 73732
  149.9 8.9 %copy-start.36 = (f32[12,512]{1,0:T(8,128)}, f32[12,512]{1,0:T(8,128)S(1)}, u32[]{:S(2)}) copy-start(f32[12,512]{1,0:T(8,128)S(1)} %fusion.15) | copy-start | bytes 73732
  150.0 8.8 %copy-start.10 = (bf16[1,512,768]{2,1,0:T(8,128)(2,1)S(1)}, bf16[1,512,768]{2,1,0:T(8,128)(2,1)}, u32[]{:S(2)}) copy-start(bf16[1,512,768]{2,1,0:T(8,128)(2,1)} %param.13) | copy-start | bytes 2359300
  150.0 8.8 %copy-start.59 = (bf16[768,768]{1,0:T(8,128)(2,1)S(1)}, bf16[768,768]{1,0:T(8,128)(2,1)}, u32[]{:S(2)}) copy-start(bf16[768,768]{1,0:T(8,128)(2,1)} %param.22) | copy-start | bytes 3538948
  173.5 41.0 %all-to-all-start = ((bf16[4,256,768]{2,1,0:T(8,128)(2,1)}), bf16[4,256,768]{2,1,0:T(8,128)(2,1)}, u32[]{:S(2)}, u32[]{:S(2)}) async-start(bf16[4,256,768]{2,1,0:T(8,128)(2,1)} %get-tuple-element.243), calls=%async_computation | async-start | bytes 3145728 | tf_op jit(solution)/shard_map/all_to_all | solution.py:207
  214.5 40.9 %all-to-all-start.2 = ((bf16[4,256,768]{2,1,0:T(8,128)(2,1)}), bf16[4,256,768]{2,1,0:T(8,128)(2,1)}, u32[]{:S(2)}, u32[]{:S(2)}) async-start(bf16[4,256,768]{2,1,0:T(8,128)(2,1)} %get-tuple-element.242), calls=%async_computation.2 | async-start | bytes 3145728 | tf_op jit(solution)/shard_map/all_to_all | solution.py:227
  255.4 41.3 %all-to-all-start.1 = ((bf16[4,256,768]{2,1,0:T(8,128)(2,1)}), bf16[4,256,768]{2,1,0:T(8,128)(2,1)}, u32[]{:S(2)}, u32[]{:S(2)}) async-start(bf16[4,256,768]{2,1,0:T(8,128)(2,1)} %fusion.77), calls=%async_computation.1 | async-start | bytes 3145728 | tf_op jit(solution)/shard_map/all_to_all | solution.py:215
  296.7 40.9 %all-to-all-start.3 = ((bf16[4,256,768]{2,1,0:T(8,128)(2,1)}), bf16[4,256,768]{2,1,0:T(8,128)(2,1)}, u32[]{:S(2)}, u32[]{:S(2)}) async-start(bf16[4,256,768]{2,1,0:T(8,128)(2,1)} %fusion.82), calls=%async_computation.3 | async-start | bytes 3145728 | tf_op jit(solution)/shard_map/all_to_all | solution.py:241
  301.1 169.0 %all-reduce.8.cloned.1.call-start = ((), (), s32[]{:S(2)}) async-start(), calls=%async_computation.5 | async-start | bytes 18874368 | tf_op jit(solution)/shard_map/psum | solution.py:304
  313.2 363.2 %all-reduce.6.cloned.1.call-start = ((), (), s32[]{:S(2)}) async-start(), calls=%async_computation.4 | async-start | bytes 18874368 | tf_op jit(solution)/shard_map/psum | solution.py:292
  318.1 24.2 %copy-start.46 = (f32[512]{0:T(512)S(1)}, f32[512]{0:T(512)}, u32[]{:S(2)}) copy-start(f32[512]{0:T(512)} %copy-done.45) | copy-start | bytes 6148
  356.2 8.6 %copy-start.17 = (bf16[512,768]{0,1:T(8,128)(2,1)S(1)}, bf16[512,768]{0,1:T(8,128)(2,1)}, u32[]{:S(2)}) copy-start(bf16[512,768]{0,1:T(8,128)(2,1)} %copy.94) | copy-start | bytes 2359300
  397.1 13.0 %collective-permute-start.2 = (bf16[512,1536]{0,1:T(8,128)(2,1)}, bf16[512,1536]{0,1:T(8,128)(2,1)}, u32[]{:S(2)}, u32[]{:S(2)}) collective-permute-start(bf16[512,1536]{0,1:T(8,128)(2,1)} %pad_maximum_fusion.1), channel_id=1, source_target_pairs={{4,0},{8,4},{12,8},{16,12},{20,16},{24,20},{28,24},{5,1},{9,5},{13... | collective-permute-start | bytes 4718600 | tf_op jit(solution)/shard_map/ppermute | solution.py:17
  404.0 15.7 %slice-start.3 = ((s8[12582912]{0:T(1024)(128)(4,1)}), s8[4194304]{0:T(1024)(128)(4,1)S(1)}, s32[]{:S(2)}) async-start(s8[12582912]{0:T(1024)(128)(4,1)} %bitcast.292), calls=%async_computation.9 | async-start | bytes 8388608
  404.0 15.7 %slice-start.4 = ((s8[12582912]{0:T(1024)(128)(4,1)}), s8[4194304]{0:T(1024)(128)(4,1)S(1)}, s32[]{:S(2)}) async-start(s8[12582912]{0:T(1024)(128)(4,1)} %bitcast.292), calls=%async_computation.10 | async-start | bytes 8388608
  413.6 24.5 %collective-permute-start.3 = (bf16[512,1536]{0,1:T(8,128)(2,1)}, bf16[512,1536]{0,1:T(8,128)(2,1)}, u32[]{:S(2)}, u32[]{:S(2)}) collective-permute-start(bf16[512,1536]{0,1:T(8,128)(2,1)} %fusion.64), channel_id=1, source_target_pairs={{4,0},{8,4},{12,8},{16,12},{20,16},{24,20},{28,24},{5,1},{9,5},{13... | collective-permute-start | bytes 4718600 | tf_op jit(solution)/shard_map/ppermute | solution.py:17
  419.8 18.4 %copy-start.14 = (f32[12,64,512]{2,1,0:T(8,128)S(1)}, f32[12,64,512]{2,1,0:T(8,128)}, u32[]{:S(2)}) copy-start(f32[12,64,512]{2,1,0:T(8,128)} %convolution_multiply_fusion) | copy-start | bytes 4718596
  423.4 17.9 %copy-start.11 = (bf16[1,512,768]{2,1,0:T(8,128)(2,1)S(1)}, bf16[1,512,768]{2,1,0:T(8,128)(2,1)}, u32[]{:S(2)}) copy-start(bf16[1,512,768]{2,1,0:T(8,128)(2,1)} %param.13) | copy-start | bytes 2359300
  423.4 17.9 %copy-start.31 = (bf16[12,64,512]{2,1,0:T(8,128)(2,1)S(1)}, bf16[12,64,512]{2,1,0:T(8,128)(2,1)}, u32[]{:S(2)}) copy-start(bf16[12,64,512]{2,1,0:T(8,128)(2,1)} %multiply_convert_fusion.4) | copy-start | bytes 2359300
  423.4 17.9 %copy-start.49 = (f32[512]{0:T(512)S(1)}, f32[512]{0:T(512)}, u32[]{:S(2)}) copy-start(f32[512]{0:T(512)} %copy-done.48) | copy-start | bytes 6148
  423.4 17.9 %copy-start.52 = (f32[512]{0:T(512)S(1)}, f32[512]{0:T(512)}, u32[]{:S(2)}) copy-start(f32[512]{0:T(512)} %copy-done.51) | copy-start | bytes 6148
  423.4 17.9 %copy-start.54 = (f32[768]{0:T(1024)S(1)}, f32[768]{0:T(1024)}, u32[]{:S(2)}) copy-start(f32[768]{0:T(1024)} %param.17) | copy-start | bytes 9220
  423.4 17.9 %copy-start.61 = (f32[768]{0:T(1024)S(1)}, f32[768]{0:T(1024)}, u32[]{:S(2)}) copy-start(f32[768]{0:T(1024)} %param.18) | copy-start | bytes 9220
  (49 other events, 252.8 us)
Sparse Core Ops, SparseCore 0:
  313.3 156.6 all-reduce.7
  477.5 198.8 all-reduce.5
where the time goes:
time: 699 us; the launch traced here: 692 us
  waiting for transfers between devices  233 us (33%)
  matrix products  196 us (28%)
  local copies, waits for them, and re-layouts  86.4 us (12%)
  other arithmetic  74.9 us (11%)
  blocking collectives  55.8 us (8%)
  starting transfers between devices  29.9 us (4%)
  between operations  15.3 us (2%)
    psum x1, waiting for transfers between devices, on_device(): lax.psum((grad_w_qkv, grad_w_out, grad_first_gain, grad_first_bias, grad_...  129 us
    psum x1, blocking collectives, on_device(): lax.psum((grad_w_qkv, grad_w_out, grad_first_gain, grad_first_bias, grad_...  55.8 us
    dot_general x3, matrix products, step(): jnp.einsum('hqk,khd->qhd', shares.astype(jnp.bfloat16), value_rows, prefe...  34.3 us
    all_to_all x1, waiting for transfers between devices, on_device(): lax.all_to_all(send, 'exp', split_axis=0, concat_axis=0, tiled=True)  28.2 us
    dot_general x3, matrix products, step(): jnp.einsum('qhd,khd->hqk', queries, key_rows, preferred_element_type=jnp....  25.3 us
    dot_general x3, matrix products, backward_core(): jnp.einsum('qhd,khd->hqk', grad_heads, value_rows, preferred_element_type...  23.4 us
    psum x1, waiting for transfers between devices, on_device(): lax.psum(grad_w_up.astype(jnp.bfloat16), 'seq').astype(jnp.float32)  23.3 us
    all_to_all x1, waiting for transfers between devices, on_device(): lax.all_to_all(grad_slots.reshape(experts_total, capacity, width), 'exp',...  19.5 us
  transfers between devices with their start and end apart: 10, of which 7 were waited for; matrix products, arithmetic and copies ran while one was open for 36% of the time, Pallas kernels for 0%

commit v1 on v0

--- a/solution.py
+++ b/solution.py
@@ -204,7 +204,19 @@
     own_start = jnp.sum(jnp.where(matches, starts[None, :], 0), axis=1)
     token_slot = choice_ids * capacity + places - own_start
     send = jnp.where(filled, ffn_in[gather_index], jnp.zeros((), jnp.bfloat16))
-    received = lax.all_to_all(send, "exp", split_axis=0, concat_axis=0, tiled=True)
+    ways, here = (lax.axis_size("exp"), lax.axis_index("exp"))
+    width_2 = send.shape[0] // ways
+    dims = list(send.shape)
+    dims[0] = width_2
+    height = dims[0]
+    dims[0] = height * ways
+    full = jnp.zeros(dims, send.dtype)
+    for mask in range(ways):
+        part = lax.dynamic_slice_in_dim(send, (here ^ mask) * width_2, width_2, axis=0)
+        if mask:
+            part = lax.ppermute(part, "exp", [(d, d ^ mask) for d in range(ways)])
+        full = lax.dynamic_update_slice_in_dim(full, part, (here ^ mask) * height, axis=0)
+    received = full
     grouped = received.reshape(sources, local_exp, capacity, width)
     pre_act = jnp.einsum("secd,edf->secf", grouped, w_up, preferred_element_type=jnp.float32)
     activated, gate_pullback = jax.vjp(smooth_gate, pre_act)

time: 699 us -> 711 us (1.017)
  starting transfers between devices: 29.9 us -> 48.5 us
    ppermute x0 -> x3, waiting for transfers between devices: none -> 37.1 us  [on_device(): part = lax.ppermute(part, 'exp', [(d, d ^ mask) for d in range(ways)])]
    all_to_all x1 -> x0, waiting for transfers between devices: 28.2 us -> none  [on_device(): lax.all_to_all(send, 'exp', split_axis=0, concat_axis=0, tiled=True)]
    all_to_all x1, starting transfers between devices: 4.78 us -> 20.2 us  [on_device(): lax.all_to_all(expert_out.reshape(experts_total, capacity, width), 'exp',...]
    all_to_all x1, waiting for transfers between devices: 13.9 us -> 0.01 us  [on_device(): lax.all_to_all(grad_send, 'exp', split_axis=0, concat_axis=0, tiled=True)]
    ppermute x0 -> x3, starting transfers between devices: none -> 8 us  [on_device(): part = lax.ppermute(part, 'exp', [(d, d ^ mask) for d in range(ways)])]
    unnamed x146 -> x156, local copies, waits for them, and re-layouts: 18.2 us -> 19.3 us
  transfers between devices with their start and end apart: 10 -> 12, of which waited for: 7 -> 8; matrix products, arithmetic and copies ran while one was open for 36% -> 35% of each run, Pallas kernels for 0% -> 0%
where the time goes in v1:
time: 711 us; the launch traced here: 704 us
  waiting for transfers between devices  229 us (32%)
  matrix products  195 us (27%)
  local copies, waits for them, and re-layouts  87 us (12%)
  other arithmetic  72.8 us (10%)
  blocking collectives  56.7 us (8%)
  starting transfers between devices  48.5 us (7%)
  between operations  15.4 us (2%)
    psum x1, waiting for transfers between devices, on_device(): lax.psum((grad_w_qkv, grad_w_out, grad_first_gain, grad_first_bias, grad_...  129 us
    psum x1, blocking collectives, on_device(): lax.psum((grad_w_qkv, grad_w_out, grad_first_gain, grad_first_bias, grad_...  56.7 us
    ppermute x3, waiting for transfers between devices, on_device(): part = lax.ppermute(part, 'exp', [(d, d ^ mask) for d in range(ways)])  37.1 us
    dot_general x3, matrix products, step(): jnp.einsum('hqk,khd->qhd', shares.astype(jnp.bfloat16), value_rows, prefe...  34.4 us
    dot_general x3, matrix products, step(): jnp.einsum('qhd,khd->hqk', queries, key_rows, preferred_element_type=jnp....  25.2 us
    dot_general x3, matrix products, backward_core(): jnp.einsum('qhd,khd->hqk', grad_heads, value_rows, preferred_element_type...  23.4 us
    psum x1, waiting for transfers between devices, on_device(): lax.psum(grad_w_up.astype(jnp.bfloat16), 'seq').astype(jnp.float32)  20.3 us
    all_to_all x1, waiting for transfers between devices, on_device(): lax.all_to_all(grad_slots.reshape(experts_total, capacity, width), 'exp',...  20.3 us
  transfers between devices with their start and end apart: 12, of which 8 were waited for; matrix products, arithmetic and copies ran while one was open for 35% of the time, Pallas kernels for 0%

profile of v1, /device:TPU:0, one launch (start us, length us, event | category | flops | bytes accessed | tf_op | source)
XLA Modules:
  0.0 704.1 jit_solution(4435883542559779204)
XLA Ops:
  31.5 6.9 gather_fusion.1
  48.4 6.8 gather_fusion.4
  64.9 8.5 %select_reduce_fusion.2 = (f32[12,512]{1,0:T(8,128)}, f32[12,512,512]{1,2,0:T(8,128)}) fusion(pred[512,512]{0,1:T(8,128)(4,1)S(1)} %get-tuple-element.243, bf16[512,12,64]{0,2,1:T(8,128)(2,1)} %bitcast.294, bf16[512,12,64]{0,2,1:T(8,128)(2,1)} %bitcast.300), kind=kOutput, calls=%fused_computation.33 | convolution fusion | flops 412084224 | bytes 14442496 | tf_op jit(solution)/shard_map/while/body/eval_jaxpr/qhd,khd->hqk/dot_general | solution.py:71
  80.6 8.6 %select_reduce_fusion.1 = (f32[12,512]{1,0:T(8,128)}, f32[12,512,512]{1,2,0:T(8,128)}) fusion(pred[512,512]{0,1:T(8,128)(4,1)} %get-tuple-element.245, bf16[512,12,64]{0,2,1:T(8,128)(2,1)} %bitcast.295, bf16[512,12,64]{0,2,1:T(8,128)(2,1)} %bitcast.302), kind=kOutput, calls=%fused_computation.31 | convolution fusion | flops 412084224 | bytes 14442496 | tf_op jit(solution)/shard_map/while/body/eval_jaxpr/qhd,khd->hqk/dot_general | solution.py:71
  96.5 8.1 %select_reduce_fusion = (f32[12,512]{1,0:T(8,128)S(1)}, f32[12,512,512]{1,2,0:T(8,128)}) fusion(pred[512,512]{0,1:T(8,128)(4,1)} %get-tuple-element.244, bf16[512,12,64]{0,2,1:T(8,128)(2,1)} %bitcast.296, bf16[512,12,64]{0,2,1:T(8,128)(2,1)} %bitcast.304), kind=kOutput, calls=%fused_computation.29 | convolution fusion | flops 412084224 | bytes 14442496 | tf_op jit(solution)/shard_map/while/body/eval_jaxpr/qhd,khd->hqk/dot_general | solution.py:71
  105.2 7.3 %fusion.13 = f32[12,512]{1,0:T(8,128)S(1)} fusion(f32[12,512,512]{1,2,0:T(8,128)} %get-tuple-element.264, f32[12,512]{1,0:T(8,128)S(1)} %get-tuple-element.210, pred[512,512]{0,1:T(8,128)(4,1)S(1)} %copy-done.20), kind=kLoop, calls=%fused_computation.36 | loop fusion | flops 12576768 | bytes 12894208 | tf_op jit(solution)/shard_map/while/body/eval_jaxpr/reduce_sum | solution.py:77
  112.6 20.9 %fusion.36 = f32[12,64,512]{2,1,0:T(8,128)} fusion(bf16[512,12,64]{0,2,1:T(8,128)(2,1)} %bitcast.324, f32[12,512,512]{1,2,0:T(8,128)} %get-tuple-element.264, f32[12,512]{1,0:T(8,128)S(1)} %get-tuple-element.210, pred[512,512]{0,1:T(8,128)(4,1)} %get-tuple-element.245), kind=kOutput, calls=%fused_computation.57 | convolution fusion | flops 415236096 | bytes 15228928 | tf_op jit(solution)/shard_map/while/body/eval_jaxpr/hqk,khd->qhd/dot_general | solution.py:78
  141.8 7.3 %fusion.15 = f32[12,512]{1,0:T(8,128)S(1)} fusion(f32[12,512,512]{1,2,0:T(8,128)} %get-tuple-element.262, f32[12,512]{1,0:T(8,128)} %get-tuple-element.196, pred[512,512]{0,1:T(8,128)(4,1)} %get-tuple-element.244), kind=kLoop, calls=%fused_computation.38 | loop fusion | flops 12576768 | bytes 12894208 | tf_op jit(solution)/shard_map/while/body/eval_jaxpr/reduce_sum | solution.py:77
  149.3 8.8 %fusion.158 = (bf16[512,12,64]{0,2,1:T(8,128)(2,1)S(1)}, f32[512,12,64]{0,2,1:T(8,128)}) fusion(f32[512,12]{0,1:T(8,128)S(1)} %get-tuple-element.194, bf16[512,12,64]{0,2,1:T(8,128)(2,1)S(1)} %bitcast.326, f32[12,512,512]{1,2,0:T(8,128)} %get-tuple-element.262, f32[12,512]{1,0:T(8,128)S(1)} %copy-done.40, pred[512,512]{0,1:T(8,128)(4,1)S(1)} %copy-done.22, ...), kind=kOutput, calls=%fused_computation.223 | convolution fusion | flops 417988608 | bytes 19259392 | tf_op jit(solution)/shard_map/while/body/eval_jaxpr/hqk,khd->qhd/dot_general | solution.py:78
  161.9 6.8 gather_fusion.2
  188.2 6.8 collective-permute-done.2
  196.8 9.0 %collective-permute-done.3 = bf16[1,256,768]{2,1,0:T(8,128)(2,1)} collective-permute-done((bf16[1,256,768]{2,1,0:T(8,128)(2,1)}, bf16[1,256,768]{2,1,0:T(8,128)(2,1)}, u32[]{:S(2)}, u32[]{:S(2)}) %collective-permute-start.3) | collective-permute-done | bytes 393248 | tf_op jit(solution)/shard_map/ppermute | solution.py:217
  207.6 21.2 %collective-permute-done.4 = bf16[1,256,768]{2,1,0:T(8,128)(2,1)S(1)} collective-permute-done((bf16[1,256,768]{2,1,0:T(8,128)(2,1)}, bf16[1,256,768]{2,1,0:T(8,128)(2,1)S(1)}, u32[]{:S(2)}, u32[]{:S(2)}) %collective-permute-start.4) | collective-permute-done | bytes 393248 | tf_op jit(solution)/shard_map/ppermute | solution.py:217
  229.6 7.3 %fusion.54 = f32[4,256,3072]{2,1,0:T(8,128)S(1)} fusion(bf16[4,256,768]{2,1,0:T(8,128)(2,1)} %constant_dynamic-update-slice_fusion, bf16[1,768,3072]{2,1,0:T(8,128)(2,1)} %param.23), kind=kOutput, calls=%fused_computation.69 | convolution fusion | flops 4831838208 | bytes 18874368 | tf_op jit(solution)/shard_map/secd,edf->secf/dot_general | solution.py:221
  241.4 10.8 %fusion.77 = bf16[4,256,768]{2,1,0:T(8,128)(2,1)} fusion(bf16[1,3072,768]{2,1,0:T(8,128)(2,1)} %param.24, f32[4,256,3072]{2,1,0:T(8,128)S(1)} %fusion.54), kind=kOutput, calls=%fused_computation.95 | convolution fusion | flops 4860936192 | bytes 18874368 | tf_op jit(solution)/shard_map/secf,efd->secd/dot_general | solution.py:224
  252.2 20.2 %all-to-all-start = ((bf16[4,256,768]{2,1,0:T(8,128)(2,1)}), bf16[4,256,768]{2,1,0:T(8,128)(2,1)}, u32[]{:S(2)}, u32[]{:S(2)}) async-start(bf16[4,256,768]{2,1,0:T(8,128)(2,1)} %fusion.77), calls=%async_computation | async-start | bytes 3145728 | tf_op jit(solution)/shard_map/all_to_all | solution.py:227
  272.4 15.3 %fusion.6 = bf16[4,1,256,3072]{3,2,0,1:T(8,128)(2,1)S(1)} fusion(f32[4,256,3072]{2,1,0:T(8,128)} %copy-done.69, bf16[4,256,768]{2,1,0:T(8,128)(2,1)} %all-to-all-done.1, bf16[1,3072,768]{2,1,0:T(8,128)(2,1)} %param.24), kind=kOutput, calls=%fused_computation.14 | convolution fusion | flops 4894752768 | bytes 25165824 | tf_op jit(solution)/shard_map/secd,efd->secf/dot_general | solution.py:245
  287.8 8.7 %fusion.82 = bf16[4,256,768]{2,1,0:T(8,128)(2,1)} fusion(bf16[1,768,3072]{2,1,0:T(8,128)(2,1)} %param.23, bf16[4,1,256,3072]{3,2,0,1:T(8,128)(2,1)S(1)} %fusion.6), kind=kOutput, calls=%fused_computation.96 | convolution fusion | flops 4832624640 | bytes 12582912 | tf_op jit(solution)/shard_map/secf,edf->secd/dot_general | solution.py:250
  296.4 6.8 fusion.56
  312.4 12.0 %fusion.59 = bf16[1,3072,768]{2,1,0:T(8,128)(2,1)} fusion(bf16[4,256,768]{2,1,0:T(8,128)(2,1)} %all-to-all-done.1, f32[4,256,3072]{2,1,0:T(8,128)} %copy-done.69), kind=kOutput, calls=%fused_computation.72 | convolution fusion | flops 4862509056 | bytes 18874368 | tf_op jit(solution)/shard_map/secf,secd->efd/dot_general | solution.py:242
  329.4 20.3 %all-to-all-done.2 = bf16[4,256,768]{2,1,0:T(8,128)(2,1)} async-done(((bf16[4,256,768]{2,1,0:T(8,128)(2,1)}), bf16[4,256,768]{2,1,0:T(8,128)(2,1)}, u32[]{:S(2)}, u32[]{:S(2)}) %all-to-all-start.2) | async-done | bytes 1572896 | tf_op jit(solution)/shard_map/all_to_all | solution.py:253
  368.4 8.6 %fusion.110 = bf16[12,64,512]{2,1,0:T(8,128)(2,1)} fusion(bf16[512,12,64]{0,2,1:T(8,128)(2,1)} %bitcast.311, f32[12,512,512]{1,2,0:T(8,128)} %get-tuple-element.262, f32[12,512]{1,0:T(8,128)} %log_add_fusion, pred[512,512]{0,1:T(8,128)(4,1)} %get-tuple-element.244), kind=kOutput, calls=%fused_computation.132 | convolution fusion | flops 415629312 | bytes 14442496 | tf_op jit(solution)/shard_map/while/body/eval_jaxpr/hqk,qhd->khd/dot_general | solution.py:126
  376.9 7.8 %multiply_convert_fusion = bf16[12,512,512]{1,2,0:T(8,128)(2,1)S(1)} fusion(f32[12,512,512]{1,2,0:T(8,128)} %get-tuple-element.262, f32[12,512]{1,0:T(8,128)S(1)} %bitcast.331, f32[12,512]{1,0:T(8,128)S(1)} %copy-done.49, pred[512,512]{0,1:T(8,128)(4,1)S(1)} %copy-done.23, bf16[512,12,64]{0,2,1:T(8,128)(2,1)S(1)} %bitcast.312, ...), kind=kOutput, calls=%fused_computation.22 | convolution fusion | flops 421527552 | bytes 20758528 | tf_op jit(solution)/shard_map/while/body/eval_jaxpr/qhd,khd->hqk/dot_general | solution.py:96
  384.8 7.6 %multiply_convert_fusion.2 = bf16[12,512,512]{1,2,0:T(8,128)(2,1)S(1)} fusion(f32[12,512,512]{1,2,0:T(8,128)} %get-tuple-element.266, f32[12,512]{1,0:T(8,128)S(1)} %bitcast.332, f32[12,512]{1,0:T(8,128)S(1)} %copy-done.49, pred[512,512]{0,1:T(8,128)(4,1)} %copy-done.19, bf16[512,12,64]{0,2,1:T(8,128)(2,1)S(1)} %bitcast.313, bf16[512,12,64]{0,2,1:T(8,128)(2,1)} %bitcast.323), kind=kOutput, calls=%fused_computation.26 | convolution fusion | flops 421527552 | bytes 20758528 | tf_op jit(solution)/shard_map/while/body/eval_jaxpr/qhd,khd->hqk/dot_general | solution.py:96
  397.9 7.9 %multiply_convert_fusion.1 = bf16[12,512,512]{1,2,0:T(8,128)(2,1)S(1)} fusion(f32[12,512,512]{1,2,0:T(8,128)} %get-tuple-element.264, f32[12,512]{1,0:T(8,128)S(1)} %bitcast.333, f32[12,512]{1,0:T(8,128)S(1)} %copy-done.49, pred[512,512]{0,1:T(8,128)(4,1)} %get-tuple-element.245, bf16[512,12,64]{0,2,1:T(8,128)(2,1)S(1)} %bitcast.314, ...), kind=kOutput, calls=%fused_computation.24 | convolution fusion | flops 421527552 | bytes 20758528 | tf_op jit(solution)/shard_map/while/body/eval_jaxpr/qhd,khd->hqk/dot_general | solution.py:96
  416.1 6.1 fusion.30
  435.5 17.2 %collective-permute-done.6 = bf16[512,1536]{0,1:T(8,128)(2,1)} collective-permute-done((bf16[512,1536]{0,1:T(8,128)(2,1)}, bf16[512,1536]{0,1:T(8,128)(2,1)}, u32[]{:S(2)}, u32[]{:S(2)}) %collective-permute-start.6) | collective-permute-done | bytes 1572896 | tf_op jit(solution)/shard_map/ppermute | solution.py:17
  461.3 20.3 %all-reduce.8.cloned.1.call-done = (bf16[1,768,3072]{2,1,0:T(8,128)(2,1)}, bf16[1,3072,768]{2,1,0:T(8,128)(2,1)}) async-done(((bf16[1,768,3072]{2,1,0:T(8,128)(2,1)}, bf16[1,3072,768]{2,1,0:T(8,128)(2,1)}), (bf16[1,768,3072]{2,1,0:T(8,128)(2,1)}, bf16[1,3072,768]{2,1,0:T(8,128)(2,1)})) %all-reduce.8.cloned.1.call-update) | async-done | bytes 9437200 | tf_op jit(solution)/shard_map/psum | solution.py:316
  481.6 7.5 %convert_element_type.162 = f32[1,768,3072]{2,1,0:T(8,128)} convert(bf16[1,768,3072]{2,1,0:T(8,128)(2,1)} %get-tuple-element.192) | non-fusion elementwise | flops 2359296 | bytes 14155776 | tf_op jit(solution)/shard_map/convert_element_type | solution.py:316
  497.8 56.7 %all-reduce = (f32[768]{0:T(1024)}, f32[768]{0:T(1024)}, f32[768]{0:T(1024)}, f32[768]{0:T(1024)}) all-reduce(f32[768]{0:T(1024)} %get-tuple-element.167, f32[768]{0:T(1024)} %get-tuple-element.170, f32[768]{0:T(1024)S(1)} %get-tuple-element.165, f32[768]{0:T(1024)S(1)} %copy-done.52), channel_id=1, replica_groups=mesh['seq'=8,'exp'=4] {'seq','exp'}, use_global_device_ids=true, to_apply=%region_23.24 | all-reduce | flops 3072 | bytes 24576 | tf_op jit(solution)/shard_map/psum | solution.py:304
  559.8 129.0 %all-reduce.6.cloned.1.call-done = (f32[768,2304]{1,0:T(8,128)}, f32[768,768]{1,0:T(8,128)}) async-done(((f32[768,2304]{1,0:T(8,128)}, f32[768,768]{1,0:T(8,128)}), (f32[768,2304]{1,0:T(8,128)}, f32[768,768]{1,0:T(8,128)})) %all-reduce.6.cloned.1.call-update) | async-done | bytes 9437200 | tf_op jit(solution)/shard_map/psum | solution.py:304
  688.8 6.6 copy.136
  (258 shorter events, 184.9 us)
Async XLA Ops:
  10.2 9.5 %copy-start.61 = (s32[1,512]{1,0:T(1,128)S(1)}, s32[1,512]{1,0:T(1,128)}, u32[]{:S(2)}) copy-start(s32[1,512]{1,0:T(1,128)} %param.14) | copy-start | bytes 6148
  16.2 43.2 %collective-permute-start = (bf16[512,1536]{1,0:T(8,128)(2,1)}, bf16[512,1536]{1,0:T(8,128)(2,1)}, u32[]{:S(2)}, u32[]{:S(2)}) collective-permute-start(bf16[512,1536]{1,0:T(8,128)(2,1)} %slice.67), channel_id=1, source_target_pairs={{0,4},{4,8},{8,12},{12,16},{16,20},{20,24},{24,28},{1,5},{5,9},{9,... | collective-permute-start | bytes 4718600 | tf_op jit(solution)/shard_map/ppermute | solution.py:17
  48.4 15.8 %copy-start.60 = (s32[4]{0:T(128)S(1)}, s32[4]{0:T(128)}, u32[]{:S(2)}) copy-start(s32[4]{0:T(128)} %copy-done.59) | copy-start | bytes 52
  59.4 14.0 %copy-start.19 = (pred[512,512]{0,1:T(8,128)(4,1)}, pred[512,512]{0,1:T(8,128)(4,1)S(1)}, u32[]{:S(2)}) copy-start(pred[512,512]{0,1:T(8,128)(4,1)S(1)} %get-tuple-element.243) | copy-start | bytes 786436
  59.4 29.8 %collective-permute-start.1 = (bf16[512,1536]{1,0:T(8,128)(2,1)}, bf16[512,1536]{1,0:T(8,128)(2,1)}, u32[]{:S(2)}, u32[]{:S(2)}) collective-permute-start(bf16[512,1536]{1,0:T(8,128)(2,1)} %collective-permute-done), channel_id=1, source_target_pairs={{0,4},{4,8},{8,12},{12,16},{16,20},{20,24},{24,28},{1,5},{5,9},{9,... | collective-permute-start | bytes 4718600 | tf_op jit(solution)/shard_map/ppermute | solution.py:17
  105.2 28.2 %slice-start = ((s8[12582912]{0:T(1024)(128)(4,1)}), s8[4194304]{0:T(1024)(128)(4,1)S(1)}, s32[]{:S(2)}) async-start(s8[12582912]{0:T(1024)(128)(4,1)} %bitcast.290), calls=%async_computation.5 | async-start | bytes 8388608
  105.2 28.2 %slice-start.1 = ((s8[12582912]{0:T(1024)(128)(4,1)}), s8[4194304]{0:T(1024)(128)(4,1)S(1)}, s32[]{:S(2)}) async-start(s8[12582912]{0:T(1024)(128)(4,1)} %bitcast.290), calls=%async_computation.6 | async-start | bytes 8388608
  112.5 36.6 %copy-start.37 = (f32[12,512]{1,0:T(8,128)}, f32[12,512]{1,0:T(8,128)S(1)}, u32[]{:S(2)}) copy-start(f32[12,512]{1,0:T(8,128)S(1)} %fusion.13) | copy-start | bytes 73732
  112.5 20.9 %slice-start.2 = ((s8[12582912]{0:T(1024)(128)(4,1)}), s8[4194304]{0:T(1024)(128)(4,1)S(1)}, s32[]{:S(2)}) async-start(s8[12582912]{0:T(1024)(128)(4,1)} %bitcast.290), calls=%async_computation.7 | async-start | bytes 8388608
  137.0 12.1 %copy-start.38 = (f32[12,512]{1,0:T(8,128)}, f32[12,512]{1,0:T(8,128)S(1)}, u32[]{:S(2)}) copy-start(f32[12,512]{1,0:T(8,128)S(1)} %fusion.11) | copy-start | bytes 73732
  149.1 8.9 %copy-start.39 = (f32[12,512]{1,0:T(8,128)}, f32[12,512]{1,0:T(8,128)S(1)}, u32[]{:S(2)}) copy-start(f32[12,512]{1,0:T(8,128)S(1)} %fusion.15) | copy-start | bytes 73732
  149.2 8.8 %copy-start.10 = (bf16[1,512,768]{2,1,0:T(8,128)(2,1)S(1)}, bf16[1,512,768]{2,1,0:T(8,128)(2,1)}, u32[]{:S(2)}) copy-start(bf16[1,512,768]{2,1,0:T(8,128)(2,1)} %param.13) | copy-start | bytes 2359300
  149.2 8.8 %copy-start.64 = (bf16[768,768]{1,0:T(8,128)(2,1)S(1)}, bf16[768,768]{1,0:T(8,128)(2,1)}, u32[]{:S(2)}) copy-start(bf16[768,768]{1,0:T(8,128)(2,1)} %param.22) | copy-start | bytes 3538948
  174.3 20.7 %collective-permute-start.2 = (bf16[1,256,768]{2,1,0:T(8,128)(2,1)}, bf16[1,256,768]{2,1,0:T(8,128)(2,1)}, u32[]{:S(2)}, u32[]{:S(2)}) collective-permute-start(bf16[1,256,768]{2,1,0:T(8,128)(2,1)} %get-tuple-element.218), channel_id=1, source_target_pairs={{0,1},{1,0},{2,3},{3,2},{4,5},{5,4},{6,7},{7,6},{8,9},{9,8},{10,11... | collective-permute-start | bytes 1179656 | tf_op jit(solution)/shard_map/ppermute | solution.py:217
  175.9 29.9 %collective-permute-start.3 = (bf16[1,256,768]{2,1,0:T(8,128)(2,1)}, bf16[1,256,768]{2,1,0:T(8,128)(2,1)}, u32[]{:S(2)}, u32[]{:S(2)}) collective-permute-start(bf16[1,256,768]{2,1,0:T(8,128)(2,1)} %get-tuple-element.217), channel_id=1, source_target_pairs={{0,2},{1,3},{2,0},{3,1},{4,6},{5,7},{6,4},{7,5},{8,10},{9,11},{10,... | collective-permute-start | bytes 1179656 | tf_op jit(solution)/shard_map/ppermute | solution.py:217
  178.6 73.6 %all-to-all-start.1 = ((bf16[4,256,768]{2,1,0:T(8,128)(2,1)}), bf16[4,256,768]{2,1,0:T(8,128)(2,1)}, u32[]{:S(2)}, u32[]{:S(2)}) async-start(bf16[4,256,768]{2,1,0:T(8,128)(2,1)} %get-tuple-element.246), calls=%async_computation.1 | async-start | bytes 3145728 | tf_op jit(solution)/shard_map/all_to_all | solution.py:239
  183.0 45.8 %collective-permute-start.4 = (bf16[1,256,768]{2,1,0:T(8,128)(2,1)}, bf16[1,256,768]{2,1,0:T(8,128)(2,1)S(1)}, u32[]{:S(2)}, u32[]{:S(2)}) collective-permute-start(bf16[1,256,768]{2,1,0:T(8,128)(2,1)} %get-tuple-element.216), channel_id=1, source_target_pairs={{0,3},{1,2},{2,1},{3,0},{4,7},{5,6},{6,5},{7,4},{8,11},{9,10},{10,... | collective-permute-start | bytes 1179656 | tf_op jit(solution)/shard_map/ppermute | solution.py:217
  252.2 55.9 %all-to-all-start = ((bf16[4,256,768]{2,1,0:T(8,128)(2,1)}), bf16[4,256,768]{2,1,0:T(8,128)(2,1)}, u32[]{:S(2)}, u32[]{:S(2)}) async-start(bf16[4,256,768]{2,1,0:T(8,128)(2,1)} %fusion.77), calls=%async_computation | async-start | bytes 3145728 | tf_op jit(solution)/shard_map/all_to_all | solution.py:227
  308.0 41.6 %all-to-all-start.2 = ((bf16[4,256,768]{2,1,0:T(8,128)(2,1)}), bf16[4,256,768]{2,1,0:T(8,128)(2,1)}, u32[]{:S(2)}, u32[]{:S(2)}) async-start(bf16[4,256,768]{2,1,0:T(8,128)(2,1)} %fusion.82), calls=%async_computation.2 | async-start | bytes 3145728 | tf_op jit(solution)/shard_map/all_to_all | solution.py:253
  312.4 169.2 %all-reduce.8.cloned.1.call-start = ((), (), s32[]{:S(2)}) async-start(), calls=%async_computation.4 | async-start | bytes 18874368 | tf_op jit(solution)/shard_map/psum | solution.py:316
  324.5 364.3 %all-reduce.6.cloned.1.call-start = ((), (), s32[]{:S(2)}) async-start(), calls=%async_computation.3 | async-start | bytes 18874368 | tf_op jit(solution)/shard_map/psum | solution.py:304
  409.1 13.1 %collective-permute-start.5 = (bf16[512,1536]{0,1:T(8,128)(2,1)}, bf16[512,1536]{0,1:T(8,128)(2,1)}, u32[]{:S(2)}, u32[]{:S(2)}) collective-permute-start(bf16[512,1536]{0,1:T(8,128)(2,1)} %pad_maximum_fusion.1), channel_id=1, source_target_pairs={{4,0},{8,4},{12,8},{16,12},{20,16},{24,20},{28,24},{5,1},{9,5},{13... | collective-permute-start | bytes 4718600 | tf_op jit(solution)/shard_map/ppermute | solution.py:17
  416.1 15.7 %slice-start.3 = ((s8[12582912]{0:T(1024)(128)(4,1)}), s8[4194304]{0:T(1024)(128)(4,1)S(1)}, s32[]{:S(2)}) async-start(s8[12582912]{0:T(1024)(128)(4,1)} %bitcast.292), calls=%async_computation.8 | async-start | bytes 8388608
  416.1 15.7 %slice-start.4 = ((s8[12582912]{0:T(1024)(128)(4,1)}), s8[4194304]{0:T(1024)(128)(4,1)S(1)}, s32[]{:S(2)}) async-start(s8[12582912]{0:T(1024)(128)(4,1)} %bitcast.292), calls=%async_computation.9 | async-start | bytes 8388608
  425.6 27.1 %collective-permute-start.6 = (bf16[512,1536]{0,1:T(8,128)(2,1)}, bf16[512,1536]{0,1:T(8,128)(2,1)}, u32[]{:S(2)}, u32[]{:S(2)}) collective-permute-start(bf16[512,1536]{0,1:T(8,128)(2,1)} %fusion.64), channel_id=1, source_target_pairs={{4,0},{8,4},{12,8},{16,12},{20,16},{24,20},{28,24},{5,1},{9,5},{13... | collective-permute-start | bytes 4718600 | tf_op jit(solution)/shard_map/ppermute | solution.py:17
  431.8 20.9 %copy-start.14 = (f32[12,64,512]{2,1,0:T(8,128)S(1)}, f32[12,64,512]{2,1,0:T(8,128)}, u32[]{:S(2)}) copy-start(f32[12,64,512]{2,1,0:T(8,128)} %convolution_multiply_fusion) | copy-start | bytes 4718596
  435.4 20.5 %copy-start.11 = (bf16[1,512,768]{2,1,0:T(8,128)(2,1)S(1)}, bf16[1,512,768]{2,1,0:T(8,128)(2,1)}, u32[]{:S(2)}) copy-start(bf16[1,512,768]{2,1,0:T(8,128)(2,1)} %param.13) | copy-start | bytes 2359300
  435.4 20.5 %copy-start.34 = (bf16[12,64,512]{2,1,0:T(8,128)(2,1)S(1)}, bf16[12,64,512]{2,1,0:T(8,128)(2,1)}, u32[]{:S(2)}) copy-start(bf16[12,64,512]{2,1,0:T(8,128)(2,1)} %multiply_convert_fusion.4) | copy-start | bytes 2359300
  435.4 20.5 %copy-start.51 = (f32[512]{0:T(512)S(1)}, f32[512]{0:T(512)}, u32[]{:S(2)}) copy-start(f32[512]{0:T(512)} %copy-done.50) | copy-start | bytes 6148
  435.5 20.5 %copy-start.54 = (f32[512]{0:T(512)S(1)}, f32[512]{0:T(512)}, u32[]{:S(2)}) copy-start(f32[512]{0:T(512)} %copy-done.53) | copy-start | bytes 6148
  435.5 20.5 %copy-start.57 = (f32[768]{0:T(1024)S(1)}, f32[768]{0:T(1024)}, u32[]{:S(2)}) copy-start(f32[768]{0:T(1024)} %param.17) | copy-start | bytes 9220
  435.5 20.4 %copy-start.66 = (f32[768]{0:T(1024)S(1)}, f32[768]{0:T(1024)}, u32[]{:S(2)}) copy-start(f32[768]{0:T(1024)} %param.18) | copy-start | bytes 9220
  (56 other events, 289.2 us)
Sparse Core Ops, SparseCore 0:
  324.6 156.8 all-reduce.7
  489.1 199.6 all-reduce.5
